TPU v7x, 32 devices: a whole 2x2x4 slice. The times are simulated.
32 devices in a mesh: layer: 8 (over z, y), latent: 4 (over x, core).
Axes of the slice: x: 2, y: 2, z: 4, core: 2. Of those that a mesh axis runs over, the one named last changes fastest.
Arguments:
- layer_inputs: bfloat16 [384, 8192], P('latent', 'layer'), may hold values from -6 to 6
- mlp_outputs: bfloat16 [384, 8192], P('latent', 'layer'), may hold values from -6 to 6
- enc_weight: bfloat16 [8192, 4096], P('layer', 'latent'), may hold values from -0.125 to 0.125
- enc_bias: float32 [4, 4096], P(None, 'latent'), may hold values from -1 to 0.5
- dec_weight: bfloat16 [4, 4096, 8192], P(None, 'latent', 'layer'), may hold values from -0.046875 to 0.046875
Outputs:
- enc_grad: float32 [8192, 4096], P('layer', 'latent')
- dec_grad: bfloat16 [4, 4096, 8192], P(None, 'latent', 'layer')
All inputs are finite; a program needn't handle non-finite values.
Results may differ from a plain program's by a relative error of at most 0.011.
Values may be sent and summed in bfloat16 or wider, within the bound.
A program may use at most 64 MiB of HBM per device.

v0:
```python
import jax
import jax.numpy as jnp
from jax import lax
from jax.sharding import PartitionSpec as P


def from_partner(x, axis, distance):
    return lax.ppermute(x, axis, [(i, i ^ 1 << distance) for i in range(lax.axis_size(axis))])


def take_layer(stack, index):
    return lax.dynamic_index_in_dim(stack, index, 0, keepdims=False)


def local(layer_inputs, mlp_outputs, enc_weight, enc_bias, dec_weight):
    position = lax.axis_index("layer")
    layer_now = position // 2
    which_half = position % 2
    inputs_half = lax.all_gather(layer_inputs, "latent", axis=0, tiled=True)
    total_rows = inputs_half.shape[0]
    half_rows = total_rows // 2
    width_half = dec_weight.shape[2]
    latent_cols = enc_weight.shape[1]
    own_part = jnp.dot(inputs_half, enc_weight, preferred_element_type=jnp.float32)
    partner = from_partner(own_part, "layer", 0)
    pre_acts = own_part + partner + take_layer(enc_bias, layer_now)[None, :]
    latents = jnp.maximum(pre_acts, 0.0).astype(jnp.bfloat16)
    own_rows = lax.dynamic_slice_in_dim(latents, which_half * half_rows, half_rows, 0)
    gathered = lax.all_gather(own_rows[None], "layer", axis=0, tiled=True)
    layer_count = gathered.shape[0] // 2
    gathered = gathered.reshape(layer_count, total_rows, latent_cols)
    upper = layer_now + 1
    rscale = total_rows ** (-0.5)

    def add_source(source, total):
        block = take_layer(gathered, source)
        return total + jnp.dot(
            block, take_layer(dec_weight, source), preferred_element_type=jnp.float32
        )

    recon_full = lax.psum(
        lax.fori_loop(0, upper, add_source, jnp.zeros((total_rows, width_half), jnp.float32)),
        "latent",
    )
    target_full = lax.all_gather(mlp_outputs, "latent", axis=0, tiled=True)
    out_grad = ((recon_full - target_full.astype(jnp.float32)) * rscale).astype(jnp.bfloat16)

    def back_source(source, carry):
        grads, lat_terms = carry
        block = take_layer(gathered, source)
        weight = take_layer(dec_weight, source)
        dec_piece = lax.dot_general(
            block, out_grad, (((0,), (0,)), ((), ())), preferred_element_type=jnp.float32
        ).astype(jnp.bfloat16)
        lat_piece = lax.dot_general(
            out_grad, weight, (((1,), (1,)), ((), ())), preferred_element_type=jnp.float32
        )
        grads = lax.dynamic_update_index_in_dim(grads, dec_piece, source, 0)
        lat_terms = lax.dynamic_update_index_in_dim(lat_terms, lat_piece, source, 0)
        return (grads, lat_terms)

    start_carry = (
        jnp.zeros(dec_weight.shape, jnp.bfloat16),
        jnp.zeros((layer_count, total_rows, latent_cols), jnp.float32),
    )
    dec_grad, lat_terms = lax.fori_loop(0, upper, back_source, start_carry)
    split_terms = lat_terms.reshape(2 * layer_count, half_rows, latent_cols)
    own_sum = lax.psum_scatter(split_terms, "layer", scatter_dimension=0, tiled=True)[0]
    own_pre = lax.dynamic_slice_in_dim(pre_acts, which_half * half_rows, half_rows, 0)
    own_grad = jnp.where(own_pre > 0.0, own_sum, 0.0).astype(jnp.bfloat16)
    partner_grad = from_partner(own_grad, "layer", 0)
    first_rows = jnp.where(which_half == 0, own_grad, partner_grad)
    second_rows = jnp.where(which_half == 0, partner_grad, own_grad)
    pre_grad = jnp.concatenate([first_rows, second_rows], axis=0)
    enc_grad = lax.dot_general(
        inputs_half, pre_grad, (((0,), (0,)), ((), ())), preferred_element_type=jnp.float32
    )
    return (enc_grad, dec_grad)


def solution(mesh):
    in_specs = (
        P("latent", "layer"),
        P("latent", "layer"),
        P("layer", "latent"),
        P(None, "latent"),
        P(None, "latent", "layer"),
    )
    out_specs = (P("layer", "latent"), P(None, "latent", "layer"))
    return jax.shard_map(local, mesh=mesh, in_specs=in_specs, out_specs=out_specs, check_vma=False)
```

profile of v0, /device:TPU:20, one launch (start us, length us, event | category | flops | bytes accessed | tf_op | source)
XLA Modules:
  0.0 391.6 jit_solution(11983994195876657834)
XLA Ops:
  7.2 8.9 %all_gather.9 = bf16[384,1024]{1,0:T(8,128)(2,1)S(1)} all-gather(bf16[96,1024]{1,0:T(8,128)(2,1)} %param.9), channel_id=1, replica_groups=mesh['layer'=8,'latent'=4] {'latent'}, dimensions={0}, use_global_device_ids=true | all-gather | bytes 983040 | tf_op jit(solution)/shard_map/all_gather | solution.py:19
  16.2 2.1 fusion.24
  19.5 35.7 %collective-permute-done = f32[384,1024]{1,0:T(8,128)} collective-permute-done((f32[384,1024]{1,0:T(8,128)}, f32[384,1024]{1,0:T(8,128)}, u32[]{:S(2)}, u32[]{:S(2)}) %collective-permute-start) | collective-permute-done | bytes 1572896 | tf_op jit(solution)/shard_map/ppermute | solution.py:8
  55.3 2.2 add_add_fusion
  59.5 59.4 %all-gather.3.cloned.1.call-done = bf16[1536,1024]{1,0:T(8,128)(2,1)} async-done(((bf16[192,1024]{1,0:T(8,128)(2,1)}), bf16[1536,1024]{1,0:T(8,128)(2,1)}) %all-gather.3.cloned.1.call-update) | async-done | bytes 3145744 | tf_op jit(solution)/shard_map/all_gather | solution.py:29
  120.2 13.2 %while.22 = (s32[]{:T(128)}, f32[384,1024]{1,0:T(8,128)}, s32[]{:T(128)}, bf16[4,384,1024]{2,1,0:T(8,128)(2,1)}, bf16[4,1024,1024]{2,1,0:T(8,128)(2,1)}, /*index=5*/s32[]{:T(128)}, s32[]{:T(128)}, s32[]{:T(128)}) while((s32[]{:T(128)}, f32[384,1024]{1,0:T(8,128)}, s32[]{:T(128)}, bf16[4,384,1024]{2,1,0:T(8,128)(2,1)}, ...), condition=%wide.region_1.2_spmd, body=%wide.region_0.1_spmd.sunk | while | flops 805699584 | bytes 6030463 | solution.py:42
  120.2 4.4 %fusion.40 = f32[384,1024]{1,0:T(8,128)} fusion(f32[384,1024]{1,0:T(8,128)} %get-tuple-element.185, bf16[4,1024,1024]{2,1,0:T(8,128)(2,1)} %get-tuple-element.196, s32[]{:T(128)S(6)} %select_n.66, bf16[4,384,1024]{2,1,0:T(8,128)(2,1)} %get-tuple-element.195), kind=kOutput, calls=%fused_computation.3.clone.1 | convolution fusion | flops 805699584 | bytes 6030336 | tf_op jit(solution)/shard_map/while/body/dot_general | solution.py:37
  124.6 4.4 %fusion.40 = f32[384,1024]{1,0:T(8,128)} fusion(f32[384,1024]{1,0:T(8,128)} %get-tuple-element.185, bf16[4,1024,1024]{2,1,0:T(8,128)(2,1)} %get-tuple-element.196, s32[]{:T(128)S(6)} %select_n.66, bf16[4,384,1024]{2,1,0:T(8,128)(2,1)} %get-tuple-element.195), kind=kOutput, calls=%fused_computation.3.clone.1 | convolution fusion | flops 805699584 | bytes 6030336 | tf_op jit(solution)/shard_map/while/body/dot_general | solution.py:37
  129.0 4.4 %fusion.40 = f32[384,1024]{1,0:T(8,128)} fusion(f32[384,1024]{1,0:T(8,128)} %get-tuple-element.185, bf16[4,1024,1024]{2,1,0:T(8,128)(2,1)} %get-tuple-element.196, s32[]{:T(128)S(6)} %select_n.66, bf16[4,384,1024]{2,1,0:T(8,128)(2,1)} %get-tuple-element.195), kind=kOutput, calls=%fused_computation.3.clone.1 | convolution fusion | flops 805699584 | bytes 6030336 | tf_op jit(solution)/shard_map/while/body/dot_general | solution.py:37
  133.5 8.6 %all_gather.11 = bf16[384,1024]{1,0:T(8,128)(2,1)S(1)} all-gather(bf16[96,1024]{1,0:T(8,128)(2,1)S(1)} %copy-done.5), channel_id=1, replica_groups=mesh['layer'=8,'latent'=4] {'latent'}, dimensions={0}, use_global_device_ids=true | all-gather | bytes 983040 | tf_op jit(solution)/shard_map/all_gather | solution.py:45
  142.1 38.8 %all-reduce.2.cloned.1.call-done = f32[384,1024]{1,0:T(8,128)} async-done(((f32[384,1024]{1,0:T(8,128)}), f32[384,1024]{1,0:T(8,128)}) %all-reduce.2.cloned.1.call-update) | async-done | bytes 1572880 | tf_op jit(solution)/shard_map/psum | solution.py:41
  180.9 2.5 multiply_convert_fusion
  183.4 3.4 broadcast_in_dim.21.clone
  186.9 4.5 %broadcast_in_dim.20 = bf16[4,1024,1024]{2,1,0:T(8,128)(2,1)} broadcast(bf16[]{:T(256)} %constant.76.clone.1), dimensions={} | broadcast | bytes 8388610 | tf_op jit(solution)/shard_map/broadcast_in_dim | solution.py:63
  191.3 40.6 %while.23 = (s32[]{:T(128)}, bf16[4,1024,1024]{2,1,0:T(8,128)(2,1)}, f32[4,384,1024]{2,1,0:T(8,128)}, s32[]{:T(128)}, bf16[4,384,1024]{2,1,0:T(8,128)(2,1)}, /*i...) while((s32[]{:T(128)}, ...), condition=%wide.region_4.5_spmd, body=%wide.region_3.4_spmd.sunk | while | flops 1611661312 | bytes 14419095 | solution.py:66
  191.3 4.0 %fusion.45 = f32[1,384,1024]{1,2,0:T(8,128)} fusion(bf16[384,1024]{1,0:T(8,128)(2,1)S(1)} %get-tuple-element.225, bf16[4,1024,1024]{2,1,0:T(8,128)(2,1)} %get-tuple-element.226, s32[]{:T(128)S(6)} %select_n.67), kind=kOutput, calls=%fused_computation.11.clone.1 | convolution fusion | flops 805306368 | bytes 4456452 | tf_op jit(solution)/shard_map/while/body/dot_general | solution.py:55
  195.3 3.0 copy.12
  198.4 2.8 constant_dynamic-update-slice_fusion.2
  201.1 3.7 bitcast_dynamic-update-slice_fusion.2
  204.9 4.0 %fusion.45 = f32[1,384,1024]{1,2,0:T(8,128)} fusion(bf16[384,1024]{1,0:T(8,128)(2,1)S(1)} %get-tuple-element.225, bf16[4,1024,1024]{2,1,0:T(8,128)(2,1)} %get-tuple-element.226, s32[]{:T(128)S(6)} %select_n.67), kind=kOutput, calls=%fused_computation.11.clone.1 | convolution fusion | flops 805306368 | bytes 4456452 | tf_op jit(solution)/shard_map/while/body/dot_general | solution.py:55
  208.9 3.0 copy.12
  211.9 2.7 constant_dynamic-update-slice_fusion.2
  214.7 3.7 bitcast_dynamic-update-slice_fusion.2
  218.4 4.0 %fusion.45 = f32[1,384,1024]{1,2,0:T(8,128)} fusion(bf16[384,1024]{1,0:T(8,128)(2,1)S(1)} %get-tuple-element.225, bf16[4,1024,1024]{2,1,0:T(8,128)(2,1)} %get-tuple-element.226, s32[]{:T(128)S(6)} %select_n.67), kind=kOutput, calls=%fused_computation.11.clone.1 | convolution fusion | flops 805306368 | bytes 4456452 | tf_op jit(solution)/shard_map/while/body/dot_general | solution.py:55
  222.4 3.0 copy.12
  225.5 2.7 constant_dynamic-update-slice_fusion.2
  228.2 3.7 bitcast_dynamic-update-slice_fusion.2
  232.0 131.1 %reduce-scatter.2.cloned.1.call-done = f32[1,192,1024]{2,1,0:T(8,128)} async-done(((f32[8,192,1024]{2,1,0:T(8,128)}), f32[1,192,1024]{2,1,0:T(8,128)}) %reduce-scatter.2.cloned.1.call-update) | async-done | bytes 786448 | tf_op jit(solution)/shard_map/reduce_scatter | solution.py:68
  363.0 1.5 fusion.22
  365.1 10.3 %collective-permute-done.1 = bf16[192,1024]{1,0:T(8,128)(2,1)} collective-permute-done((bf16[192,1024]{1,0:T(8,128)(2,1)S(1)}, bf16[192,1024]{1,0:T(8,128)(2,1)}, u32[]{:S(2)}, u32[]{:S(2)}) %collective-permute-start.1) | collective-permute-done | bytes 393248 | tf_op jit(solution)/shard_map/ppermute | solution.py:8
  376.5 3.2 convolution_bitcast_fusion
  379.8 5.3 %copy.8 = f32[1024,1024]{1,0:T(8,128)} copy(f32[1024,1024]{0,1:T(8,128)} %convolution_bitcast_fusion) | data formatting | bytes 8388608
  (24 shorter events, 6.4 us)
Async XLA Ops:
  7.2 9.0 %copy-start = (bf16[1024,1024]{1,0:T(8,128)(2,1)S(1)}, bf16[1024,1024]{1,0:T(8,128)(2,1)}, u32[]{:S(2)}) copy-start(bf16[1024,1024]{1,0:T(8,128)(2,1)} %param.11) | copy-start | bytes 6291460
  7.2 111.7 %all-gather.3.cloned.1.call-start = ((), (), s32[]{:S(2)}) async-start(), calls=%async_computation.3 | async-start | bytes 3538944 | tf_op jit(solution)/shard_map/all_gather | solution.py:29
  16.2 2.1 copy-start.2
  18.3 37.0 %collective-permute-start = (f32[384,1024]{1,0:T(8,128)}, f32[384,1024]{1,0:T(8,128)}, u32[]{:S(2)}, u32[]{:S(2)}) collective-permute-start(f32[384,1024]{1,0:T(8,128)} %fusion.24), channel_id=1, source_target_pairs={{0,4},{4,0},{8,12},{12,8},{16,20},{20,16},{24,28},{28,24},{1,5},{5... | collective-permute-start | bytes 4718600 | tf_op jit(solution)/shard_map/ppermute | solution.py:8
  57.4 1.1 copy-start.1
  59.4 121.5 %all-reduce.2.cloned.1.call-start = ((), (), s32[]{:S(2)}) async-start(), calls=%async_computation.1 | async-start | bytes 3145728 | tf_op jit(solution)/shard_map/psum | solution.py:41
  120.2 13.3 %copy-start.5 = (bf16[96,1024]{1,0:T(8,128)(2,1)S(1)}, bf16[96,1024]{1,0:T(8,128)(2,1)}, u32[]{:S(2)}) copy-start(bf16[96,1024]{1,0:T(8,128)(2,1)} %param.10) | copy-start | bytes 589828
  133.5 229.6 %reduce-scatter.2.cloned.1.call-start = ((), (), s32[]{:S(2)}) async-start(), calls=%async_computation.2 | async-start | bytes 7077888 | tf_op jit(solution)/shard_map/reduce_scatter | solution.py:68
  186.9 4.5 %copy-start.4 = (bf16[384,1024]{1,0:T(8,128)(2,1)S(1)}, bf16[384,1024]{1,0:T(8,128)(2,1)}, u32[]{:S(2)}) copy-start(bf16[384,1024]{1,0:T(8,128)(2,1)} %multiply_convert_fusion) | copy-start | bytes 2359300
  232.0 144.5 %copy-start.3 = (bf16[384,1024]{1,0:T(8,128)(2,1)S(1)}, bf16[384,1024]{1,0:T(8,128)(2,1)}, u32[]{:S(2)}) copy-start(bf16[384,1024]{1,0:T(8,128)(2,1)} %copy-done.2) | copy-start | bytes 2359300
  364.5 10.9 %collective-permute-start.1 = (bf16[192,1024]{1,0:T(8,128)(2,1)S(1)}, bf16[192,1024]{1,0:T(8,128)(2,1)}, u32[]{:S(2)}, u32[]{:S(2)}) collective-permute-start(bf16[192,1024]{1,0:T(8,128)(2,1)S(1)} %fusion.22), channel_id=1, source_target_pairs={{0,4},{4,0},{8,12},{12,8},{16,20},{20,16},{24,28},{28,24},{1,5},{5... | collective-permute-start | bytes 1179656 | tf_op jit(solution)/shard_map/ppermute | solution.py:8
Sparse Core Ops, SparseCore 0:
  59.5 59.2 all-gather.2
  133.6 47.2 all-reduce.1
  232.1 130.9 reduce-scatter.1
where the time goes:
time: 394 us; the launch traced here: 392 us
  waiting for transfers between devices  275 us (70%)
  matrix products  41.8 us (11%)
  local copies, waits for them, and re-layouts  33.8 us (9%)
  blocking collectives  17.5 us (4%)
  between operations  13.8 us (4%)
  other arithmetic  8.04 us (2%)
    reduce_scatter x1, waiting for transfers between devices, local(): lax.psum_scatter(split_terms, 'layer', scatter_dimension=0, tiled=True)[0]  131 us
    all_gather x1, waiting for transfers between devices, local(): gathered = lax.all_gather(own_rows[None], 'layer', axis=0, tiled=True)  59.4 us
    ppermute x2, waiting for transfers between devices, from_partner(): lax.ppermute(x, axis, [(i, i ^ 1 << distance) for i in range(lax.axis_siz...  46.1 us
    psum x1, waiting for transfers between devices, local(): lax.psum(lax.fori_loop(0, upper, add_source, jnp.zeros((total_rows, width...  38.8 us
    dynamic_update_slice x6, local copies, waits for them, and re-layouts, back_source(): lat_terms = lax.dynamic_update_index_in_dim(lat_terms, lat_piece, source, 0)  17.4 us
    dot_general x3, matrix products, add_source(): jnp.dot(block, take_layer(dec_weight, source), preferred_element_type=jnp...  13.2 us
    dot_general x3, matrix products, back_source(): lax.dot_general(out_grad, weight, (((1,), (1,)), ((), ())), preferred_ele...  12 us
    dot_general x3, matrix products, back_source(): lax.dot_general(block, out_grad, (((0,), (0,)), ((), ())), preferred_elem...  11.2 us
  transfers between devices with their start and end apart: 5, of which 5 were waited for; matrix products, arithmetic and copies ran while one was open for 0% of the time, Pallas kernels for 0%

commit v1 on v0

v1 whole, which is shorter than its diff:
```python
import functools

import jax
import jax.numpy as jnp
from jax import lax
from jax.experimental import pallas as pl
from jax.experimental.pallas import tpu as pltpu
from jax.sharding import PartitionSpec as P

MESH = pl.DeviceIdType.MESH
F32 = jnp.float32
BF16 = jnp.bfloat16


def exchange_kernel(
    layers, blocks, rscale,
    x_ref, mlp_ref, w_hbm, bias_ref, v_hbm,
    lat_out, og_out, xg_out, pg_out,
    xg, w, v, part_send, part_recv, pre, lat, recon, rs_send, rs_recv, og,
    bys, byr, bown, bzs, bzr, pg,
    x_ss, x_rs, p_ss, p_rs, z_ss, z_rs, y_ss, y_rs, rs_ss, rs_rs, og_ss, og_fs, og_rs,
    by_ss, by_rs, bz_ss, bz_rs, f_ss, f_rs, w_sem, v_sem, lat_sem, out_sem,
):
    p = lax.axis_index("layer")
    q = lax.axis_index("latent")
    t = p // 2
    y = p % 2
    o = 1 - y
    rb, depth = x_ref.shape
    half = w.shape[1] // 2
    partner = (p + 1 - 2 * y, q)
    up = (p + 2, q)
    down = (p - 2, q)
    chips = blocks // 2

    def blk(k):
        return ((q // 2 + k // 2) % chips) * 2 + (q % 2 + k % 2) % 2

    def rows(b):
        return pl.ds(pl.multiple_of(b * rb, rb), rb)

    def cols(h):
        return pl.ds(pl.multiple_of(h * half, half), half)

    def rcopy(src, dst, ss, rs, dev):
        return pltpu.make_async_remote_copy(
            src_ref=src, dst_ref=dst, send_sem=ss, recv_sem=rs, device_id=dev, device_id_type=MESH
        )

    w_copy = pltpu.make_async_copy(w_hbm, w, w_sem)
    w_copy.start()
    v_copy = pltpu.make_async_copy(v_hbm, v, v_sem)
    v_copy.start()

    barrier = pltpu.get_barrier_semaphore()
    for k in range(1, blocks):
        pl.semaphore_signal(barrier, inc=1, device_id=(p, blk(k)), device_id_type=MESH)
    pl.semaphore_signal(barrier, inc=1, device_id=partner, device_id_type=MESH)

    @pl.when(t < layers - 1)
    def _():
        pl.semaphore_signal(barrier, inc=1, device_id=up, device_id_type=MESH)

    @pl.when(t > 0)
    def _():
        pl.semaphore_signal(barrier, inc=1, device_id=down, device_id_type=MESH)

    neighbours = blocks + (t < layers - 1).astype(jnp.int32) + (t > 0).astype(jnp.int32)
    pl.semaphore_wait(barrier, neighbours)

    def x_copy(k):
        return rcopy(x_ref, xg.at[rows(q)], x_ss.at[k], x_rs.at[q], (p, blk(k)))

    for k in list(range(2, blocks)) + [1]:
        x_copy(k).start()
    xg[rows(q), :] = x_ref[...]

    def part_copy(b):
        return rcopy(part_send.at[rows(b)], part_recv.at[rows(b)], p_ss.at[b], p_rs.at[b], partner)

    def lat_up(l, b):
        piece = lat.at[l, y, rows(b)]
        return rcopy(piece, piece, z_ss.at[l, b], z_rs.at[l, b], up)

    def lat_swap(l, b):
        piece = lat.at[l, y, rows(b)]
        return rcopy(piece, piece, y_ss.at[l, b], y_rs.at[l, b], partner)

    def lat_swap_in(l, b):
        piece = lat.at[l, o, rows(b)]
        return rcopy(piece, piece, y_ss.at[l, b], y_rs.at[l, b], partner)

    def own_block(b):
        part_copy(b).wait_recv()
        total = pre[rows(b), :] + part_recv[rows(b), :] + bias
        pre[rows(b), :] = total
        lat[t, y, rows(b), :] = jnp.maximum(total, 0.0).astype(BF16)

        @pl.when(t < layers - 1)
        def _():
            lat_up(t, b).start()

        lat_swap(t, b).start()

    bias_half = jnp.where(y == 0, bias_ref[:, :half], bias_ref[:, half:])
    own_row = lax.broadcasted_iota(jnp.int32, bias_half.shape, 0) == t
    bias = jnp.sum(jnp.where(own_row, bias_half, 0.0), axis=0, keepdims=True)
    w_copy.wait()
    for k in range(blocks):
        b = blk(k)
        if k > 0:
            rcopy(x_ref, xg.at[rows(b)], x_ss.at[k], x_rs.at[b], (p, b)).wait_recv()
        part_send[rows(b), :] = jnp.dot(xg[rows(b), :], w[:, cols(o)], preferred_element_type=F32)
        part_copy(b).start()
        pre[rows(b), :] = jnp.dot(xg[rows(b), :], w[:, cols(y)], preferred_element_type=F32)
        if k > 0:
            own_block(blk(k - 1))
    own_block(blk(blocks - 1))
    xg_copy = pltpu.make_async_copy(xg, xg_out, out_sem.at[0])
    xg_copy.start()

    recon[...] = jnp.zeros_like(recon)
    v_copy.wait()

    def decode(l, h):
        recon[...] += jnp.dot(lat[l, h], v[l, cols(h), :], preferred_element_type=F32)

    def forward(s, carry):
        l = t - s

        @pl.when(jnp.logical_and(s > 0, s <= t))
        def _():
            for k in range(blocks):
                b = blk(k)
                lat_up(l, b).wait_recv()

                @pl.when(t < layers - 1)
                def _():
                    lat_up(l, b).start()

                lat_swap(l, b).start()

        @pl.when(s <= t)
        def _():
            decode(l, y)

        @pl.when(s > 0)
        def _():
            for k in range(blocks):
                lat_swap_in(l + 1, blk(k)).wait_recv()
            decode(l + 1, o)

        return carry

    lax.fori_loop(0, t + 2, forward, 0)

    def rs_copy(k):
        return rcopy(rs_send.at[k], rs_recv.at[q], rs_ss.at[k], rs_rs.at[q], (p, blk(k)))

    order = list(range(2, blocks)) + [1]
    for k in order:
        rs_send[k] = recon[rows(blk(k)), :].astype(BF16)
        rs_copy(k).start()
    total = recon[rows(q), :]
    for k in order[-1:] + order[:-1]:
        b = blk(k)
        rcopy(rs_send.at[k], rs_recv.at[b], rs_ss.at[k], rs_rs.at[b], (p, b)).wait_recv()
        total = total + rs_recv[b].astype(F32)
    og[rows(q), :] = ((total - mlp_ref[...].astype(F32)) * rscale).astype(BF16)

    def og_copy(src, ss, k):
        return rcopy(og.at[rows(src)], og.at[rows(src)], ss.at[k], og_rs.at[src], (p, blk(k)))

    def og_relay(k):
        return rcopy(og.at[rows(blk(k))], og.at[rows(blk(k))], og_fs.at[k], og_rs.at[blk(k)], (p, blk(1)))

    for k in list(range(2, blocks, 2)) + [1]:
        og_copy(q, og_ss, k).start()
    for k in range(2, blocks, 2):
        og_copy(blk(k), og_ss, k).wait_recv()
        og_relay(k).start()
    for k in range(1, blocks, 2):
        og_copy(blk(k), og_ss, k).wait_recv()
    og_dma = pltpu.make_async_copy(og, og_out, out_sem.at[1])
    og_dma.start()

    def lat_dma(l):
        return pltpu.make_async_copy(lat.at[l], lat_out.at[l], lat_sem.at[l])

    def by_copy(l, b):
        return rcopy(bys.at[l, rows(b)], byr.at[l, rows(b)], by_ss.at[l, b], by_rs.at[l, b], partner)

    def bz_copy(l, b):
        return rcopy(bzs.at[l, rows(b)], bzr.at[l, rows(b)], bz_ss.at[l, b], bz_rs.at[l, b], down)

    def back(l, h):
        return lax.dot_general(
            og[...], v[l, cols(h), :], (((1,), (1,)), ((), ())), preferred_element_type=F32
        )

    def produce(l, carry):
        bys[l] = back(l, o).astype(BF16)
        for b in range(blocks):
            by_copy(l, b).start()
        bown[l] = back(l, y)
        lat_dma(l).start()
        return carry

    lax.fori_loop(0, t + 1, produce, 0)

    def collected(l, b):
        by_copy(l, b).wait_recv()

        @pl.when(t < layers - 1)
        def _():
            bz_copy(l, b).wait_recv()
            bown[l, rows(b), :] += bzr[l, rows(b), :].astype(F32)

        return bown[l, rows(b), :] + byr[l, rows(b), :].astype(F32)

    def combine(l, carry):
        for b in range(blocks):
            bzs[l, rows(b), :] = collected(l, b).astype(BF16)
            bz_copy(l, b).start()
        return carry

    lax.fori_loop(0, t, combine, 0)

    def final_copy(h, b):
        piece = pg.at[h, rows(b)]
        return rcopy(piece, piece, f_ss.at[b], f_rs.at[b], partner)

    for b in range(blocks):
        value = jnp.where(pre[rows(b), :] > 0.0, collected(t, b), 0.0)
        pg[y, rows(b), :] = value.astype(BF16)
        final_copy(y, b).start()
    for b in range(blocks):
        final_copy(o, b).wait_recv()
    pg_dma = pltpu.make_async_copy(pg, pg_out, out_sem.at[2])
    pg_dma.start()

    for k in range(1, blocks):
        x_copy(k).wait_send()
        rs_copy(k).wait_send()
    for k in list(range(2, blocks, 2)) + [1]:
        og_copy(q, og_ss, k).wait_send()
    for k in range(2, blocks, 2):
        og_relay(k).wait_send()
    for b in range(blocks):
        part_copy(b).wait_send()
        final_copy(y, b).wait_send()

    def drain(l, carry):
        lat_dma(l).wait()
        for b in range(blocks):
            lat_swap(l, b).wait_send()
            by_copy(l, b).wait_send()

            @pl.when(t < layers - 1)
            def _():
                lat_up(l, b).wait_send()

            @pl.when(l < t)
            def _():
                bz_copy(l, b).wait_send()

        return carry

    lax.fori_loop(0, t + 1, drain, 0)
    xg_copy.wait()
    og_dma.wait()
    pg_dma.wait()


def exchange(layer_inputs, mlp_outputs, enc_weight, enc_bias, dec_weight):
    layers, latents, width = dec_weight.shape
    blocks = lax.axis_size("latent")
    rb, depth = layer_inputs.shape
    total_rows = rb * blocks
    half = latents // 2
    rscale = total_rows ** (-0.5)
    vmem = pl.BlockSpec(memory_space=pltpu.VMEM)
    anywhere = pl.BlockSpec(memory_space=pl.ANY)
    dma = pltpu.SemaphoreType.DMA
    per_block = dma((blocks,))
    per_layer = dma((layers, blocks))
    return pl.pallas_call(
        functools.partial(exchange_kernel, layers, blocks, rscale),
        out_shape=(
            jax.ShapeDtypeStruct((layers, 2, total_rows, half), BF16),
            jax.ShapeDtypeStruct((total_rows, width), BF16),
            jax.ShapeDtypeStruct((total_rows, depth), BF16),
            jax.ShapeDtypeStruct((2, total_rows, half), BF16),
        ),
        in_specs=[vmem, vmem, anywhere, vmem, anywhere],
        out_specs=(anywhere,) * 4,
        scratch_shapes=[
            pltpu.VMEM((total_rows, depth), BF16),
            pltpu.VMEM((depth, latents), BF16),
            pltpu.VMEM((layers, latents, width), BF16),
            pltpu.VMEM((total_rows, half), F32),
            pltpu.VMEM((total_rows, half), F32),
            pltpu.VMEM((total_rows, half), F32),
            pltpu.VMEM((layers, 2, total_rows, half), BF16),
            pltpu.VMEM((total_rows, width), F32),
            pltpu.VMEM((blocks, rb, width), BF16),
            pltpu.VMEM((blocks, rb, width), BF16),
            pltpu.VMEM((total_rows, width), BF16),
            pltpu.VMEM((layers, total_rows, half), BF16),
            pltpu.VMEM((layers, total_rows, half), BF16),
            pltpu.VMEM((layers, total_rows, half), F32),
            pltpu.VMEM((layers, total_rows, half), BF16),
            pltpu.VMEM((layers, total_rows, half), BF16),
            pltpu.VMEM((2, total_rows, half), BF16),
            per_block, per_block, per_block, per_block,
            per_layer, per_layer, per_layer, per_layer,
            per_block, per_block, per_block, per_block, per_block,
            per_layer, per_layer, per_layer, per_layer,
            per_block, per_block,
            dma, dma, dma((layers,)), dma((3,)),
        ],
        compiler_params=pltpu.CompilerParams(
            collective_id=0, has_side_effects=True, vmem_limit_bytes=48 * 2**20
        ),
        name="exchange",
    )(layer_inputs, mlp_outputs, enc_weight, enc_bias, dec_weight)


def transposed_dot(a, b):
    return lax.dot_general(a, b, (((0,), (0,)), ((), ())), preferred_element_type=F32)


def dec_kernel(lat_ref, og_ref, out_ref):
    layer_now = lax.axis_index("layer") // 2
    source = pl.program_id(0)

    @pl.when(source <= layer_now)
    def _():
        out_ref[0] = transposed_dot(lat_ref[0, 0], og_ref[...]).astype(BF16)

    @pl.when(source > layer_now)
    def _():
        out_ref[...] = jnp.zeros_like(out_ref)


def enc_kernel(x_ref, pg_ref, out_ref):
    out_ref[...] = transposed_dot(x_ref[...], pg_ref[0])


def local(layer_inputs, mlp_outputs, enc_weight, enc_bias, dec_weight):
    lat, og, xg, pg = exchange(layer_inputs, mlp_outputs, enc_weight, enc_bias, dec_weight)
    layers, _, total_rows, half = lat.shape
    width = og.shape[1]
    depth = xg.shape[1]
    dec_grad = pl.pallas_call(
        dec_kernel,
        grid=(layers, 2),
        in_specs=[
            pl.BlockSpec((1, 1, total_rows, half), lambda l, h: (l, h, 0, 0)),
            pl.BlockSpec((total_rows, width), lambda l, h: (0, 0)),
        ],
        out_specs=pl.BlockSpec((1, half, width), lambda l, h: (l, h, 0)),
        out_shape=jax.ShapeDtypeStruct(dec_weight.shape, BF16),
        name="dec_grad",
    )(lat, og)
    enc_grad = pl.pallas_call(
        enc_kernel,
        grid=(2, 2),
        in_specs=[
            pl.BlockSpec((total_rows, depth // 2), lambda h, i: (0, i)),
            pl.BlockSpec((1, total_rows, half), lambda h, i: (h, 0, 0)),
        ],
        out_specs=pl.BlockSpec((depth // 2, half), lambda h, i: (i, h)),
        out_shape=jax.ShapeDtypeStruct(enc_weight.shape, F32),
        name="enc_grad",
    )(xg, pg)
    return (enc_grad, dec_grad)


def solution(mesh):
    in_specs = (
        P("latent", "layer"),
        P("latent", "layer"),
        P("layer", "latent"),
        P(None, "latent"),
        P(None, "latent", "layer"),
    )
    out_specs = (P("layer", "latent"), P(None, "latent", "layer"))
    return jax.shard_map(local, mesh=mesh, in_specs=in_specs, out_specs=out_specs, check_vma=False)
```

time: 394 us -> 141 us (0.36)
  the two profiles are of different devices: /device:TPU:20 before, /device:TPU:28 now
where the time goes in v1:
time: 141 us
  Pallas kernels  134 us (95%)
  local copies, waits for them, and re-layouts  6.8 us (5%)
    pallas_call x1, Pallas kernels, exchange(): pl.pallas_call(functools.partial(exchange_kernel, layers, blocks, rscale)...  118 us
    pallas_call x1, Pallas kernels, local(): pl.pallas_call(dec_kernel, grid=(layers, 2), in_specs=[pl.BlockSpec((1, 1...  10.2 us
    unnamed x14, local copies, waits for them, and re-layouts  6.8 us
    pallas_call x1, Pallas kernels, local(): pl.pallas_call(enc_kernel, grid=(2, 2), in_specs=[pl.BlockSpec((total_row...  5.19 us

profile of v1, /device:TPU:28, one launch (start us, length us, event | category | flops | bytes accessed | tf_op | source)
XLA Modules:
  0.0 141.0 jit_solution(9124802128655877754)
XLA Ops:
  0.6 0.0 copy-start
  0.6 1.6 %copy-done = bf16[1024,1024]{1,0:T(8,128)(2,1)S(1)} copy-done((bf16[1024,1024]{1,0:T(8,128)(2,1)S(1)}, bf16[1024,1024]{1,0:T(8,128)(2,1)}, u32[]{:S(2)}) %copy-start) | copy-done | bytes 2097176
  2.2 0.0 copy-start.4
  2.2 0.9 copy-done.4
  3.2 0.0 copy-start.5
  3.2 0.9 copy-done.5
  4.1 0.0 copy-start.6
  4.1 0.7 copy-done.6
  4.8 118.2 %exchange.1 = (bf16[4,2,384,512]{3,2,1,0:T(8,128)(2,1)}, bf16[384,1024]{1,0:T(8,128)(2,1)S(1)}, bf16[384,1024]{1,0:T(8,128)(2,1)S(1)}, bf16[2,384,512]{2,1,0:T(8,128)(2,1)S(1)}) custom-call(bf16[96,1024]{1,0:T(8,128)(2,1)S(1)} %copy-done.4, bf16[96,1024]{1,0:T(8,128)(2,1)S(1)} %copy-done.5, bf16[1024,1024]{1,0:T(8,128)(2,1)S(1)} %copy-done, ...), custom_call_target="tpu_custom_call" | custom-call | tf_op jit(solution)/shard_map/exchange/pallas_call | solution.py:287
  123.0 0.0 copy-start.1
  123.0 0.9 copy-done.1
  123.9 0.0 copy-start.2
  123.9 0.9 copy-done.2
  124.8 0.0 copy-start.3
  124.8 0.9 copy-done.3
  125.6 10.2 %dec_grad.1 = bf16[4,1024,1024]{2,1,0:T(8,128)(2,1)} custom-call(bf16[4,2,384,512]{3,2,1,0:T(8,128)(2,1)} %get-tuple-element.8.lat_ref, bf16[384,1024]{1,0:T(8,128)(2,1)} %copy-done.1), custom_call_target="tpu_custom_call" | custom-call | tf_op jit(solution)/shard_map/dec_grad/pallas_call | solution.py:355
  135.8 5.2 %enc_grad.1 = f32[1024,1024]{1,0:T(8,128)} custom-call(bf16[384,1024]{1,0:T(8,128)(2,1)} %copy-done.2, bf16[2,384,512]{2,1,0:T(8,128)(2,1)} %copy-done.3), custom_call_target="tpu_custom_call" | custom-call | tf_op jit(solution)/shard_map/enc_grad/pallas_call | solution.py:366
Async XLA Ops:
  0.6 1.6 %copy-start = (bf16[1024,1024]{1,0:T(8,128)(2,1)S(1)}, bf16[1024,1024]{1,0:T(8,128)(2,1)}, u32[]{:S(2)}) copy-start(bf16[1024,1024]{1,0:T(8,128)(2,1)} %w_hbm.1) | copy-start | bytes 6291460
  2.2 0.9 copy-start.4
  3.2 0.9 copy-start.5
  4.1 0.7 copy-start.6
  123.0 0.9 copy-start.1
  123.9 0.9 copy-start.2
  124.8 0.9 copy-start.3

commit v2 on v1

v2 whole, which is shorter than its diff:
```python
import functools

import jax
import jax.numpy as jnp
from jax import lax
from jax.experimental import pallas as pl
from jax.experimental.pallas import tpu as pltpu
from jax.sharding import PartitionSpec as P

MESH = pl.DeviceIdType.MESH
F32 = jnp.float32
BF16 = jnp.bfloat16


def exchange_kernel(
    layers, blocks, rscale,
    x_hbm, mlp_hbm, w_hbm, bias_hbm, v_hbm,
    dec_out, xg_out, pg_out,
    xg, mlp, w, bias_all, v, part_send, part_recv, pre, lat, recon, rs_send, rs_recv, og,
    bys, byr, bown, bof, bzs, bzr, bzso, bzro, pg, dec,
    x_ss, x_rs, p_ss, p_rs, z_ss, z_rs, zo_ss, zo_rs, y_ss, y_rs, rs_ss, rs_rs, og_ss, og_fs, og_rs,
    by_ss, by_rs, bz_ss, bz_rs, bzo_ss, bzo_rs, f_ss, f_rs, in_sem, dec_sem, out_sem,
):
    p = lax.axis_index("layer")
    q = lax.axis_index("latent")
    t = p // 2
    y = p % 2
    o = 1 - y
    rb = x_hbm.shape[0]
    half = w.shape[1] // 2
    partner = (p + 1 - 2 * y, q)
    up = (p + 2, q)
    down = (p - 2, q)
    chips = blocks // 2

    def blk(k):
        return ((q // 2 + k // 2) % chips) * 2 + (q % 2 + k % 2) % 2

    def rows(b):
        return pl.ds(pl.multiple_of(b * rb, rb), rb)

    def cols(h):
        return pl.ds(pl.multiple_of(h * half, half), half)

    def rcopy(src, dst, ss, rs, dev):
        return pltpu.make_async_remote_copy(
            src_ref=src, dst_ref=dst, send_sem=ss, recv_sem=rs, device_id=dev, device_id_type=MESH
        )

    own_x = pltpu.make_async_copy(x_hbm, xg.at[rows(q)], in_sem.at[0])
    w_copy = pltpu.make_async_copy(w_hbm, w, in_sem.at[1])
    bias_copy = pltpu.make_async_copy(bias_hbm, bias_all, in_sem.at[2])
    mlp_copy = pltpu.make_async_copy(mlp_hbm, mlp, in_sem.at[3])
    v_copy = pltpu.make_async_copy(v_hbm, v, in_sem.at[4])
    for copy in (own_x, w_copy, bias_copy, mlp_copy, v_copy):
        copy.start()
    both_up = list(range(blocks // 2, blocks))
    one_up = list(range(blocks // 2))
    both_down = list(range(blocks - max(blocks // 4, 1), blocks))
    one_down = list(range(blocks - max(blocks // 4, 1)))

    barrier = pltpu.get_barrier_semaphore()
    for k in range(1, blocks):
        pl.semaphore_signal(barrier, inc=1, device_id=(p, blk(k)), device_id_type=MESH)
    pl.semaphore_signal(barrier, inc=1, device_id=partner, device_id_type=MESH)

    @pl.when(t < layers - 1)
    def _():
        pl.semaphore_signal(barrier, inc=1, device_id=up, device_id_type=MESH)

    @pl.when(t > 0)
    def _():
        pl.semaphore_signal(barrier, inc=1, device_id=down, device_id_type=MESH)

    neighbours = blocks + (t < layers - 1).astype(jnp.int32) + (t > 0).astype(jnp.int32)
    pl.semaphore_wait(barrier, neighbours)

    def x_copy(k):
        return rcopy(x_hbm, xg.at[rows(q)], x_ss.at[k], x_rs.at[q], (p, blk(k)))

    for k in list(range(2, blocks)) + [1]:
        x_copy(k).start()

    def part_copy(b):
        return rcopy(part_send.at[rows(b)], part_recv.at[rows(b)], p_ss.at[b], p_rs.at[b], partner)

    def lat_up(l, b):
        piece = lat.at[l, y, rows(b)]
        return rcopy(piece, piece, z_ss.at[l, b], z_rs.at[l, b], up)

    def lat_up_other(l, b):
        piece = lat.at[l, o, rows(b)]
        return rcopy(piece, piece, zo_ss.at[l, b], zo_rs.at[l, b], up)

    def lat_swap(l, b):
        piece = lat.at[l, y, rows(b)]
        return rcopy(piece, piece, y_ss.at[l, b], y_rs.at[l, b], partner)

    def lat_swap_in(l, b):
        piece = lat.at[l, o, rows(b)]
        return rcopy(piece, piece, y_ss.at[l, b], y_rs.at[l, b], partner)

    def own_block(b):
        part_copy(b).wait_recv()
        total = pre[rows(b), :] + part_recv[rows(b), :] + bias
        pre[rows(b), :] = total
        lat[t, y, rows(b), :] = jnp.maximum(total, 0.0).astype(BF16)

        @pl.when(t < layers - 1)
        def _():
            lat_up(t, b).start()

        lat_swap(t, b).start()

    bias_copy.wait()
    bias_half = jnp.where(y == 0, bias_all[:, :half], bias_all[:, half:])
    own_row = lax.broadcasted_iota(jnp.int32, bias_half.shape, 0) == t
    bias = jnp.sum(jnp.where(own_row, bias_half, 0.0), axis=0, keepdims=True)
    own_x.wait()
    w_copy.wait()
    for k in range(blocks):
        b = blk(k)
        if k > 0:
            rcopy(x_hbm, xg.at[rows(b)], x_ss.at[k], x_rs.at[b], (p, b)).wait_recv()
        part_send[rows(b), :] = jnp.dot(xg[rows(b), :], w[:, cols(o)], preferred_element_type=F32)
        part_copy(b).start()
        pre[rows(b), :] = jnp.dot(xg[rows(b), :], w[:, cols(y)], preferred_element_type=F32)
        if k > 0:
            own_block(blk(k - 1))
    own_block(blk(blocks - 1))
    xg_copy = pltpu.make_async_copy(xg, xg_out, out_sem.at[0])
    xg_copy.start()

    recon[...] = jnp.zeros_like(recon)
    v_copy.wait()

    def decode(l, h):
        recon[...] += jnp.dot(lat[l, h], v[l, cols(h), :], preferred_element_type=F32)

    def other_up(l, b):
        @pl.when(t < layers - 1)
        def _():
            lat_up_other(l, b).start()

    for k in both_up:
        b = blk(k)
        lat_swap_in(t, b).wait_recv()
        other_up(t, b)

    def forward(s, carry):
        l = t - s

        @pl.when(jnp.logical_and(s > 0, s <= t))
        def _():
            for k in range(blocks):
                b = blk(k)
                lat_up(l, b).wait_recv()

                @pl.when(t < layers - 1)
                def _():
                    lat_up(l, b).start()

                if k in one_up:
                    lat_swap(l, b).start()
            for k in both_up:
                b = blk(k)
                lat_up_other(l, b).wait_recv()
                other_up(l, b)

        @pl.when(s <= t)
        def _():
            decode(l, y)

        @pl.when(s > 0)
        def _():
            for k in one_up:
                lat_swap_in(l + 1, blk(k)).wait_recv()
            decode(l + 1, o)

        return carry

    lax.fori_loop(0, t + 2, forward, 0)

    def rs_copy(k):
        return rcopy(rs_send.at[k], rs_recv.at[q], rs_ss.at[k], rs_rs.at[q], (p, blk(k)))

    mlp_copy.wait()
    order = list(range(2, blocks)) + [1]
    for k in order:
        rs_send[k] = recon[rows(blk(k)), :].astype(BF16)
        rs_copy(k).start()
    total = recon[rows(q), :]
    for k in order[-1:] + order[:-1]:
        b = blk(k)
        rcopy(rs_send.at[k], rs_recv.at[b], rs_ss.at[k], rs_rs.at[b], (p, b)).wait_recv()
        total = total + rs_recv[b].astype(F32)
    og[rows(q), :] = ((total - mlp[...].astype(F32)) * rscale).astype(BF16)

    def og_copy(src, ss, k):
        return rcopy(og.at[rows(src)], og.at[rows(src)], ss.at[k], og_rs.at[src], (p, blk(k)))

    def og_relay(k):
        return rcopy(og.at[rows(blk(k))], og.at[rows(blk(k))], og_fs.at[k], og_rs.at[blk(k)], (p, blk(1)))

    for k in list(range(2, blocks, 2)) + [1]:
        og_copy(q, og_ss, k).start()
    for k in range(2, blocks, 2):
        og_copy(blk(k), og_ss, k).wait_recv()
        og_relay(k).start()
    for k in range(1, blocks, 2):
        og_copy(blk(k), og_ss, k).wait_recv()

    def by_copy(l, b):
        return rcopy(bys.at[l, rows(b)], byr.at[l, rows(b)], by_ss.at[l, b], by_rs.at[l, b], partner)

    def bz_copy(l, b):
        return rcopy(bzs.at[l, rows(b)], bzr.at[l, rows(b)], bz_ss.at[l, b], bz_rs.at[l, b], down)

    def bz_other(l, b):
        return rcopy(bzso.at[l, rows(b)], bzro.at[l, rows(b)], bzo_ss.at[l, b], bzo_rs.at[l, b], down)

    def dec_copy(l):
        return pltpu.make_async_copy(dec.at[l], dec_out.at[l], dec_sem.at[l])

    def back(l, h):
        return lax.dot_general(
            og[...], v[l, cols(h), :], (((1,), (1,)), ((), ())), preferred_element_type=F32
        )

    def add_own(l, b):
        bz_copy(l, b).wait_recv()
        bown[l, rows(b), :] += bzr[l, rows(b), :].astype(F32)

    def add_other(l, b):
        bz_other(l, b).wait_recv()
        bof[l, rows(b), :] += bzro[l, rows(b), :].astype(F32)

    def send_both(l, b):
        bzs[l, rows(b), :] = bown[l, rows(b), :].astype(BF16)
        bz_copy(l, b).start()
        bzso[l, rows(b), :] = bof[l, rows(b), :].astype(BF16)
        bz_other(l, b).start()

    def swap_sum(l, b):
        bys[l, rows(b), :] = bof[l, rows(b), :].astype(BF16)
        by_copy(l, b).start()

    def produce(l, carry):
        bof[l] = back(l, o)
        for k in one_down:
            swap_sum(l, blk(k))
        bown[l] = back(l, y)

        @pl.when(t == layers - 1)
        def _():
            for k in both_down:
                b = blk(k)

                @pl.when(l < t)
                def _():
                    send_both(l, b)

                @pl.when(l == t)
                def _():
                    swap_sum(l, b)

        return carry

    lax.fori_loop(0, t + 1, produce, 0)

    def collected(l, b):
        by_copy(l, b).wait_recv()
        return bown[l, rows(b), :] + byr[l, rows(b), :].astype(F32)

    def dec_piece(l):
        for h in range(2):
            piece = lax.dot_general(
                lat[l, h], og[...], (((0,), (0,)), ((), ())), preferred_element_type=F32
            )
            dec[l, h * half:(h + 1) * half, :] = piece.astype(BF16)
        dec_copy(l).start()

    def combine(l, carry):
        @pl.when(l < t)
        def _():
            @pl.when(t < layers - 1)
            def _():
                for k in both_down:
                    b = blk(k)
                    add_own(l, b)
                    add_other(l, b)
                    send_both(l, b)

            for k in one_down:
                b = blk(k)

                @pl.when(t < layers - 1)
                def _():
                    add_own(l, b)

                bzs[l, rows(b), :] = collected(l, b).astype(BF16)
                bz_copy(l, b).start()

        dec_piece(l)
        return carry

    lax.fori_loop(0, t + 1, combine, 0)

    def final_copy(h, b):
        piece = pg.at[h, rows(b)]
        return rcopy(piece, piece, f_ss.at[b], f_rs.at[b], partner)

    @pl.when(t < layers - 1)
    def _():
        for k in both_down:
            b = blk(k)
            add_own(t, b)
            add_other(t, b)
            swap_sum(t, b)

    for k in one_down + both_down:
        b = blk(k)
        if k in one_down:
            @pl.when(t < layers - 1)
            def _():
                add_own(t, b)

        value = jnp.where(pre[rows(b), :] > 0.0, collected(t, b), 0.0)
        pg[y, rows(b), :] = value.astype(BF16)
        final_copy(y, b).start()
    for b in range(blocks):
        final_copy(o, b).wait_recv()
    pg_dma = pltpu.make_async_copy(pg, pg_out, out_sem.at[1])
    pg_dma.start()

    for k in range(1, blocks):
        x_copy(k).wait_send()
        rs_copy(k).wait_send()
    for k in list(range(2, blocks, 2)) + [1]:
        og_copy(q, og_ss, k).wait_send()
    for k in range(2, blocks, 2):
        og_relay(k).wait_send()
    for b in range(blocks):
        part_copy(b).wait_send()
        final_copy(y, b).wait_send()

    def drain(l, carry):
        dec_copy(l).wait()
        for k in range(blocks):
            b = blk(k)

            @pl.when(jnp.logical_or(l == t, k in one_up))
            def _():
                lat_swap(l, b).wait_send()

            @pl.when(jnp.logical_or(l == t, k in one_down))
            def _():
                by_copy(l, b).wait_send()

            @pl.when(t < layers - 1)
            def _():
                lat_up(l, b).wait_send()
                if k in both_up:
                    lat_up_other(l, b).wait_send()

            @pl.when(l < t)
            def _():
                bz_copy(l, b).wait_send()
                if k in both_down:
                    bz_other(l, b).wait_send()

        return carry

    lax.fori_loop(0, t + 1, drain, 0)
    xg_copy.wait()
    pg_dma.wait()


def exchange(layer_inputs, mlp_outputs, enc_weight, enc_bias, dec_weight):
    layers, latents, width = dec_weight.shape
    blocks = lax.axis_size("latent")
    rb, depth = layer_inputs.shape
    total_rows = rb * blocks
    half = latents // 2
    rscale = total_rows ** (-0.5)
    hbm = pl.BlockSpec(memory_space=pltpu.HBM)
    dma = pltpu.SemaphoreType.DMA
    per_block = dma((blocks,))
    per_layer = dma((layers, blocks))
    sums = pltpu.VMEM((layers, total_rows, half), F32)
    sent = pltpu.VMEM((layers, total_rows, half), BF16)
    one_half = pltpu.VMEM((total_rows, half), F32)
    row_blocks = pltpu.VMEM((blocks, rb, width), BF16)
    return pl.pallas_call(
        functools.partial(exchange_kernel, layers, blocks, rscale),
        out_shape=(
            jax.ShapeDtypeStruct((layers, latents, width), BF16),
            jax.ShapeDtypeStruct((total_rows, depth), BF16),
            jax.ShapeDtypeStruct((2, total_rows, half), BF16),
        ),
        in_specs=[hbm] * 5,
        out_specs=(hbm,) * 3,
        scratch_shapes=[
            pltpu.VMEM((total_rows, depth), BF16),
            pltpu.VMEM((rb, width), BF16),
            pltpu.VMEM((depth, latents), BF16),
            pltpu.VMEM((layers, latents), F32),
            pltpu.VMEM((layers, latents, width), BF16),
            one_half, one_half, one_half,
            pltpu.VMEM((layers, 2, total_rows, half), BF16),
            pltpu.VMEM((total_rows, width), F32),
            row_blocks, row_blocks,
            pltpu.VMEM((total_rows, width), BF16),
            sent, sent, sums, sums, sent, sent, sent, sent,
            pltpu.VMEM((2, total_rows, half), BF16),
            pltpu.VMEM((layers, latents, width), BF16),
            per_block, per_block, per_block, per_block,
            per_layer, per_layer, per_layer, per_layer, per_layer, per_layer,
            per_block, per_block, per_block, per_block, per_block,
            per_layer, per_layer, per_layer, per_layer, per_layer, per_layer,
            per_block, per_block,
            dma((5,)), dma((layers,)), dma((2,)),
        ],
        compiler_params=pltpu.CompilerParams(
            collective_id=0, has_side_effects=True, vmem_limit_bytes=56 * 2**20
        ),
        name="exchange",
    )(layer_inputs, mlp_outputs, enc_weight, enc_bias, dec_weight)


def transposed_dot(a, b):
    return lax.dot_general(a, b, (((0,), (0,)), ((), ())), preferred_element_type=F32)


def finish_kernel(x_ref, pg_ref, dec_ref, enc_out, dec_out):
    layer_now = lax.axis_index("layer") // 2
    source = pl.program_id(1)
    enc_out[...] = transposed_dot(x_ref[...], pg_ref[0])

    @pl.when(source <= layer_now)
    def _():
        dec_out[...] = dec_ref[...]

    @pl.when(source > layer_now)
    def _():
        dec_out[...] = jnp.zeros_like(dec_out)


def local(layer_inputs, mlp_outputs, enc_weight, enc_bias, dec_weight):
    dec, xg, pg = exchange(layer_inputs, mlp_outputs, enc_weight, enc_bias, dec_weight)
    layers, latents, width = dec.shape
    total_rows, depth = xg.shape
    half = latents // 2
    piece = depth // layers
    return pl.pallas_call(
        finish_kernel,
        grid=(2, layers),
        in_specs=[
            pl.BlockSpec((total_rows, piece), lambda h, l: (0, l)),
            pl.BlockSpec((1, total_rows, half), lambda h, l: (h, 0, 0)),
            pl.BlockSpec((1, half, width), lambda h, l: (l, h, 0)),
        ],
        out_specs=(
            pl.BlockSpec((piece, half), lambda h, l: (l, h)),
            pl.BlockSpec((1, half, width), lambda h, l: (l, h, 0)),
        ),
        out_shape=(
            jax.ShapeDtypeStruct(enc_weight.shape, F32),
            jax.ShapeDtypeStruct(dec_weight.shape, BF16),
        ),
        name="finish",
    )(xg, pg, dec)


def solution(mesh):
    in_specs = (
        P("latent", "layer"),
        P("latent", "layer"),
        P("layer", "latent"),
        P(None, "latent"),
        P(None, "latent", "layer"),
    )
    out_specs = (P("layer", "latent"), P(None, "latent", "layer"))
    return jax.shard_map(local, mesh=mesh, in_specs=in_specs, out_specs=out_specs, check_vma=False)
```

time: 141 us -> 136 us (0.965)
  the two profiles are of different devices: /device:TPU:28 before, /device:TPU:20 now
where the time goes in v2:
time: 136 us; the launch traced here: 134 us
  Pallas kernels  134 us (99%)
    pallas_call x1, Pallas kernels, exchange(): pl.pallas_call(functools.partial(exchange_kernel, layers, blocks, rscale)...  122 us
    pallas_call x1, Pallas kernels, local(): pl.pallas_call(finish_kernel, grid=(2, layers), in_specs=[pl.BlockSpec((t...  12 us

profile of v2, /device:TPU:20, one launch (start us, length us, event | category | flops | bytes accessed | tf_op | source)
XLA Modules:
  0.0 134.4 jit_solution(374662799931350759)
XLA Ops:
  0.6 121.7 %exchange.1 = (bf16[4,1024,1024]{2,1,0:T(8,128)(2,1)}, bf16[384,1024]{1,0:T(8,128)(2,1)}, bf16[2,384,512]{2,1,0:T(8,128)(2,1)}) custom-call(bf16[96,1024]{1,0:T(8,128)(2,1)} %x_hbm.1, bf16[96,1024]{1,0:T(8,128)(2,1)} %mlp_hbm.1, bf16[1024,1024]{1,0:T(8,128)(2,1)} %w_hbm.1, f32[4,1024]{1,0:T(4,128)} %bias_hbm.1, bf16[4,1024,1024]{2,1,0:T(8,128)(2,1)} %v_hbm.1), custom_call_target="tpu_custom_call" | custom-call | tf_op jit(solution)/shard_map/exchange/pallas_call | solution.py:394
  122.4 12.0 %finish.1 = (f32[1024,1024]{1,0:T(8,128)}, bf16[4,1024,1024]{2,1,0:T(8,128)(2,1)}) custom-call(bf16[384,1024]{1,0:T(8,128)(2,1)} %get-tuple-element.5.x_ref, bf16[2,384,512]{2,1,0:T(8,128)(2,1)} %get-tuple-element.6.pg_ref, bf16[4,1024,1024]{2,1,0:T(8,128)(2,1)} %get-tuple-element.7.dec_ref), custom_call_target="tpu_custom_call" | custom-call | tf_op jit(solution)/shard_map/finish/pallas_call | solution.py:455

commit v3 on v2

--- a/solution.py
+++ b/solution.py
@@ -16,9 +16,9 @@
     layers, blocks, rscale,
     x_hbm, mlp_hbm, w_hbm, bias_hbm, v_hbm,
     dec_out, xg_out, pg_out,
-    xg, mlp, w, bias_all, v, part_send, part_recv, pre, lat, recon, rs_send, rs_recv, og,
+    xg, mlp, w, bias_all, v, part_send, part_recv, pre, lat, recon, core_send, core_recv, rs_send, rs_recv, og,
     bys, byr, bown, bof, bzs, bzr, bzso, bzro, pg, dec,
-    x_ss, x_rs, p_ss, p_rs, z_ss, z_rs, zo_ss, zo_rs, y_ss, y_rs, rs_ss, rs_rs, og_ss, og_fs, og_rs,
+    x_ss, x_rs, p_ss, p_rs, z_ss, z_rs, zo_ss, zo_rs, y_ss, y_rs, core_ss, core_rs, rs_ss, rs_rs, og_ss, og_fs, og_rs,
     by_ss, by_rs, bz_ss, bz_rs, bzo_ss, bzo_rs, f_ss, f_rs, in_sem, dec_sem, out_sem,
 ):
     p = lax.axis_index("layer")
@@ -142,11 +142,6 @@
         def _():
             lat_up_other(l, b).start()
 
-    for k in both_up:
-        b = blk(k)
-        lat_swap_in(t, b).wait_recv()
-        other_up(t, b)
-
     def forward(s, carry):
         l = t - s
 
@@ -162,17 +157,25 @@
 
                 if k in one_up:
                     lat_swap(l, b).start()
+
+        @pl.when(s <= t)
+        def _():
+            decode(l, y)
+
+        @pl.when(s > 0)
+        def _():
             for k in both_up:
                 b = blk(k)
-                lat_up_other(l, b).wait_recv()
-                other_up(l, b)
-
-        @pl.when(s <= t)
-        def _():
-            decode(l, y)
-
-        @pl.when(s > 0)
-        def _():
+
+                @pl.when(s == 1)
+                def _():
+                    lat_swap_in(t, b).wait_recv()
+
+                @pl.when(s > 1)
+                def _():
+                    lat_up_other(l + 1, b).wait_recv()
+
+                other_up(l + 1, b)
             for k in one_up:
                 lat_swap_in(l + 1, blk(k)).wait_recv()
             decode(l + 1, o)
@@ -181,19 +184,30 @@
 
     lax.fori_loop(0, t + 2, forward, 0)
 
-    def rs_copy(k):
-        return rcopy(rs_send.at[k], rs_recv.at[q], rs_ss.at[k], rs_rs.at[q], (p, blk(k)))
-
+    def core_copy(c):
+        return rcopy(core_send.at[c], core_recv.at[c], core_ss.at[c], core_rs.at[c], (p, blk(1)))
+
+    def rs_copy(c):
+        return rcopy(rs_send.at[c], rs_recv.at[q // 2], rs_ss.at[c], rs_rs.at[q // 2], (p, blk(2 * c)))
+
+    def rs_in(c):
+        chip = (q // 2 + c) % chips
+        return rcopy(rs_send.at[c], rs_recv.at[chip], rs_ss.at[c], rs_rs.at[chip], (p, blk(2 * c)))
+
+    order = list(range(1, chips)) + [0]
+    for c in order:
+        core_send[c] = recon[rows(blk(2 * c + 1)), :].astype(BF16)
+        core_copy(c).start()
+    for c in order:
+        core_copy(c).wait_recv()
+        total = recon[rows(blk(2 * c)), :] + core_recv[c].astype(F32)
+        if c > 0:
+            rs_send[c] = total.astype(BF16)
+            rs_copy(c).start()
     mlp_copy.wait()
-    order = list(range(2, blocks)) + [1]
-    for k in order:
-        rs_send[k] = recon[rows(blk(k)), :].astype(BF16)
-        rs_copy(k).start()
-    total = recon[rows(q), :]
-    for k in order[-1:] + order[:-1]:
-        b = blk(k)
-        rcopy(rs_send.at[k], rs_recv.at[b], rs_ss.at[k], rs_rs.at[b], (p, b)).wait_recv()
-        total = total + rs_recv[b].astype(F32)
+    for c in range(1, chips):
+        rs_in(c).wait_recv()
+        total = total + rs_recv[(q // 2 + c) % chips].astype(F32)
     og[rows(q), :] = ((total - mlp[...].astype(F32)) * rscale).astype(BF16)
 
     def og_copy(src, ss, k):
@@ -306,6 +320,13 @@
 
     lax.fori_loop(0, t + 1, combine, 0)
 
+    def blank(l, carry):
+        dec[l] = jnp.zeros((2 * half, dec.shape[2]), BF16)
+        dec_copy(l).start()
+        return carry
+
+    lax.fori_loop(t + 1, layers, blank, 0)
+
     def final_copy(h, b):
         piece = pg.at[h, rows(b)]
         return rcopy(piece, piece, f_ss.at[b], f_rs.at[b], partner)
@@ -330,12 +351,17 @@
         final_copy(y, b).start()
     for b in range(blocks):
         final_copy(o, b).wait_recv()
-    pg_dma = pltpu.make_async_copy(pg, pg_out, out_sem.at[1])
-    pg_dma.start()
+    own_dma = pltpu.make_async_copy(pg.at[y], pg_out.at[:, cols(y)], out_sem.at[1])
+    other_dma = pltpu.make_async_copy(pg.at[o], pg_out.at[:, cols(o)], out_sem.at[2])
+    own_dma.start()
+    other_dma.start()
 
     for k in range(1, blocks):
         x_copy(k).wait_send()
-        rs_copy(k).wait_send()
+    for c in range(chips):
+        core_copy(c).wait_send()
+        if c > 0:
+            rs_copy(c).wait_send()
     for k in list(range(2, blocks, 2)) + [1]:
         og_copy(q, og_ss, k).wait_send()
     for k in range(2, blocks, 2):
@@ -345,7 +371,6 @@
         final_copy(y, b).wait_send()
 
     def drain(l, carry):
-        dec_copy(l).wait()
         for k in range(blocks):
             b = blk(k)
 
@@ -372,8 +397,11 @@
         return carry
 
     lax.fori_loop(0, t + 1, drain, 0)
+    for l in range(layers):
+        dec_copy(l).wait()
     xg_copy.wait()
-    pg_dma.wait()
+    own_dma.wait()
+    other_dma.wait()
 
 
 def exchange(layer_inputs, mlp_outputs, enc_weight, enc_bias, dec_weight):
@@ -390,16 +418,17 @@
     sums = pltpu.VMEM((layers, total_rows, half), F32)
     sent = pltpu.VMEM((layers, total_rows, half), BF16)
     one_half = pltpu.VMEM((total_rows, half), F32)
-    row_blocks = pltpu.VMEM((blocks, rb, width), BF16)
+    row_blocks = pltpu.VMEM((blocks // 2, rb, width), BF16)
+    per_chip = dma((blocks // 2,))
     return pl.pallas_call(
         functools.partial(exchange_kernel, layers, blocks, rscale),
         out_shape=(
             jax.ShapeDtypeStruct((layers, latents, width), BF16),
             jax.ShapeDtypeStruct((total_rows, depth), BF16),
-            jax.ShapeDtypeStruct((2, total_rows, half), BF16),
+            jax.ShapeDtypeStruct((total_rows, latents), BF16),
         ),
         in_specs=[hbm] * 5,
-        out_specs=(hbm,) * 3,
+        out_specs=(pl.BlockSpec(memory_space=pl.ANY),) * 3,
         scratch_shapes=[
             pltpu.VMEM((total_rows, depth), BF16),
             pltpu.VMEM((rb, width), BF16),
@@ -409,17 +438,17 @@
             one_half, one_half, one_half,
             pltpu.VMEM((layers, 2, total_rows, half), BF16),
             pltpu.VMEM((total_rows, width), F32),
-            row_blocks, row_blocks,
+            row_blocks, row_blocks, row_blocks, row_blocks,
             pltpu.VMEM((total_rows, width), BF16),
             sent, sent, sums, sums, sent, sent, sent, sent,
             pltpu.VMEM((2, total_rows, half), BF16),
             pltpu.VMEM((layers, latents, width), BF16),
             per_block, per_block, per_block, per_block,
             per_layer, per_layer, per_layer, per_layer, per_layer, per_layer,
-            per_block, per_block, per_block, per_block, per_block,
+            per_chip, per_chip, per_chip, per_chip, per_block, per_block, per_block,
             per_layer, per_layer, per_layer, per_layer, per_layer, per_layer,
             per_block, per_block,
-            dma((5,)), dma((layers,)), dma((2,)),
+            dma((5,)), dma((layers,)), dma((3,)),
         ],
         compiler_params=pltpu.CompilerParams(
             collective_id=0, has_side_effects=True, vmem_limit_bytes=56 * 2**20
@@ -428,48 +457,10 @@
     )(layer_inputs, mlp_outputs, enc_weight, enc_bias, dec_weight)
 
 
-def transposed_dot(a, b):
-    return lax.dot_general(a, b, (((0,), (0,)), ((), ())), preferred_element_type=F32)
-
-
-def finish_kernel(x_ref, pg_ref, dec_ref, enc_out, dec_out):
-    layer_now = lax.axis_index("layer") // 2
-    source = pl.program_id(1)
-    enc_out[...] = transposed_dot(x_ref[...], pg_ref[0])
-
-    @pl.when(source <= layer_now)
-    def _():
-        dec_out[...] = dec_ref[...]
-
-    @pl.when(source > layer_now)
-    def _():
-        dec_out[...] = jnp.zeros_like(dec_out)
-
-
 def local(layer_inputs, mlp_outputs, enc_weight, enc_bias, dec_weight):
-    dec, xg, pg = exchange(layer_inputs, mlp_outputs, enc_weight, enc_bias, dec_weight)
-    layers, latents, width = dec.shape
-    total_rows, depth = xg.shape
-    half = latents // 2
-    piece = depth // layers
-    return pl.pallas_call(
-        finish_kernel,
-        grid=(2, layers),
-        in_specs=[
-            pl.BlockSpec((total_rows, piece), lambda h, l: (0, l)),
-            pl.BlockSpec((1, total_rows, half), lambda h, l: (h, 0, 0)),
-            pl.BlockSpec((1, half, width), lambda h, l: (l, h, 0)),
-        ],
-        out_specs=(
-            pl.BlockSpec((piece, half), lambda h, l: (l, h)),
-            pl.BlockSpec((1, half, width), lambda h, l: (l, h, 0)),
-        ),
-        out_shape=(
-            jax.ShapeDtypeStruct(enc_weight.shape, F32),
-            jax.ShapeDtypeStruct(dec_weight.shape, BF16),
-        ),
-        name="finish",
-    )(xg, pg, dec)
+    dec_grad, xg, pg = exchange(layer_inputs, mlp_outputs, enc_weight, enc_bias, dec_weight)
+    enc_grad = lax.dot_general(xg, pg, (((0,), (0,)), ((), ())), preferred_element_type=F32)
+    return (enc_grad, dec_grad)
 
 
 def solution(mesh):

time: 136 us -> 133 us (0.978)
  Pallas kernels: 134 us -> 119 us
  local copies, waits for them, and re-layouts: 0 us -> 7.76 us
  matrix products: 0 us -> 4.68 us
    pallas_call x1 -> x0, Pallas kernels: 12 us -> none  [local(): pl.pallas_call(finish_kernel, grid=(2, layers), in_specs=[pl.BlockSpec((t...]
    unnamed x0 -> x1, local copies, waits for them, and re-layouts: none -> 7.76 us
    dot_general x0 -> x1, matrix products: none -> 4.68 us  [local(): lax.dot_general(xg, pg, (((0,), (0,)), ((), ())), preferred_element_type=...]
    pallas_call x1, Pallas kernels: 122 us -> 119 us  [exchange(): pl.pallas_call(functools.partial(exchange_kernel, layers, blocks, rscale)...]
where the time goes in v3:
time: 133 us; the launch traced here: 132 us
  Pallas kernels  119 us (89%)
  local copies, waits for them, and re-layouts  7.76 us (6%)
  matrix products  4.68 us (4%)
    pallas_call x1, Pallas kernels, exchange(): pl.pallas_call(functools.partial(exchange_kernel, layers, blocks, rscale)...  119 us
    unnamed x1, local copies, waits for them, and re-layouts  7.76 us
    dot_general x1, matrix products, local(): lax.dot_general(xg, pg, (((0,), (0,)), ((), ())), preferred_element_type=...  4.68 us

profile of v3, /device:TPU:20, one launch (start us, length us, event | category | flops | bytes accessed | tf_op | source)
XLA Modules:
  0.0 132.3 jit_solution(3096365141602547332)
XLA Ops:
  0.6 119.3 %exchange.1 = (bf16[4,1024,1024]{2,1,0:T(8,128)(2,1)}, bf16[384,1024]{1,0:T(8,128)(2,1)}, bf16[384,1024]{1,0:T(8,128)(2,1)}) custom-call(bf16[96,1024]{1,0:T(8,128)(2,1)} %x_hbm.1, bf16[96,1024]{1,0:T(8,128)(2,1)} %mlp_hbm.1, bf16[1024,1024]{1,0:T(8,128)(2,1)} %w_hbm.1, f32[4,1024]{1,0:T(4,128)} %bias_hbm.1, bf16[4,1024,1024]{2,1,0:T(8,128)(2,1)} %v_hbm.1), custom_call_target="tpu_custom_call" | custom-call | tf_op jit(solution)/shard_map/exchange/pallas_call | solution.py:423
  119.9 4.7 %fusion = f32[1024,1024]{1,0:T(8,128)} fusion(bf16[384,1024]{1,0:T(8,128)(2,1)} %get-tuple-element.5, bf16[384,1024]{1,0:T(8,128)(2,1)} %get-tuple-element.6), kind=kOutput, calls=%fused_computation | convolution fusion | flops 805306368 | bytes 5767168 | tf_op jit(solution)/shard_map/dot_general | solution.py:462
  124.6 7.8 %copy.8 = bf16[4,1024,1024]{2,1,0:T(8,128)(2,1)} copy(bf16[4,1024,1024]{2,1,0:T(8,128)(2,1)} %get-tuple-element.11) | data formatting | bytes 16777216

commit v4 on v3

--- a/solution.py
+++ b/solution.py
@@ -112,6 +112,22 @@
 
         lat_swap(t, b).start()
 
+    def relay(l, k):
+        b = blk(k)
+        lat_up(l, b).wait_recv()
+
+        @pl.when(t < layers - 1)
+        def _():
+            lat_up(l, b).start()
+
+        if k in one_up:
+            lat_swap(l, b).start()
+
+    def relay_below(k):
+        @pl.when(t > 0)
+        def _():
+            relay(t - 1, k)
+
     bias_copy.wait()
     bias_half = jnp.where(y == 0, bias_all[:, :half], bias_all[:, half:])
     own_row = lax.broadcasted_iota(jnp.int32, bias_half.shape, 0) == t
@@ -127,7 +143,11 @@
         pre[rows(b), :] = jnp.dot(xg[rows(b), :], w[:, cols(y)], preferred_element_type=F32)
         if k > 0:
             own_block(blk(k - 1))
+        if k > 1:
+            relay_below(k - 2)
     own_block(blk(blocks - 1))
+    relay_below(blocks - 2)
+    relay_below(blocks - 1)
     xg_copy = pltpu.make_async_copy(xg, xg_out, out_sem.at[0])
     xg_copy.start()
 
@@ -145,18 +165,10 @@
     def forward(s, carry):
         l = t - s
 
-        @pl.when(jnp.logical_and(s > 0, s <= t))
+        @pl.when(jnp.logical_and(s > 1, s <= t))
         def _():
             for k in range(blocks):
-                b = blk(k)
-                lat_up(l, b).wait_recv()
-
-                @pl.when(t < layers - 1)
-                def _():
-                    lat_up(l, b).start()
-
-                if k in one_up:
-                    lat_swap(l, b).start()
+                relay(l, k)
 
         @pl.when(s <= t)
         def _():
@@ -294,17 +306,29 @@
             dec[l, h * half:(h + 1) * half, :] = piece.astype(BF16)
         dec_copy(l).start()
 
+    def combine_both(l, carry):
+        for k in both_down:
+            b = blk(k)
+            add_own(l, b)
+            add_other(l, b)
+
+            @pl.when(l < t)
+            def _():
+                send_both(l, b)
+
+            @pl.when(l == t)
+            def _():
+                swap_sum(l, b)
+
+        return carry
+
+    @pl.when(t < layers - 1)
+    def _():
+        lax.fori_loop(0, t + 1, combine_both, 0)
+
     def combine(l, carry):
         @pl.when(l < t)
         def _():
-            @pl.when(t < layers - 1)
-            def _():
-                for k in both_down:
-                    b = blk(k)
-                    add_own(l, b)
-                    add_other(l, b)
-                    send_both(l, b)
-
             for k in one_down:
                 b = blk(k)
 
@@ -331,15 +355,7 @@
         piece = pg.at[h, rows(b)]
         return rcopy(piece, piece, f_ss.at[b], f_rs.at[b], partner)
 
-    @pl.when(t < layers - 1)
-    def _():
-        for k in both_down:
-            b = blk(k)
-            add_own(t, b)
-            add_other(t, b)
-            swap_sum(t, b)
-
-    for k in one_down + both_down:
+    for k in both_down + one_down:
         b = blk(k)
         if k in one_down:
             @pl.when(t < layers - 1)

time: 133 us -> 128 us (0.962)
  Pallas kernels: 119 us -> 115 us
    pallas_call x1, Pallas kernels: 119 us -> 115 us  [exchange(): pl.pallas_call(functools.partial(exchange_kernel, layers, blocks, rscale)...]
where the time goes in v4:
time: 128 us
  Pallas kernels  115 us (90%)
  local copies, waits for them, and re-layouts  7.76 us (6%)
  matrix products  4.68 us (4%)
    pallas_call x1, Pallas kernels, exchange(): pl.pallas_call(functools.partial(exchange_kernel, layers, blocks, rscale)...  115 us
    unnamed x1, local copies, waits for them, and re-layouts  7.76 us
    dot_general x1, matrix products, local(): lax.dot_general(xg, pg, (((0,), (0,)), ((), ())), preferred_element_type=...  4.68 us

profile of v4, /device:TPU:20, one launch (start us, length us, event | category | flops | bytes accessed | tf_op | source)
XLA Modules:
  0.0 128.1 jit_solution(13694549439624901518)
XLA Ops:
  0.6 115.1 %exchange.1 = (bf16[4,1024,1024]{2,1,0:T(8,128)(2,1)}, bf16[384,1024]{1,0:T(8,128)(2,1)}, bf16[384,1024]{1,0:T(8,128)(2,1)}) custom-call(bf16[96,1024]{1,0:T(8,128)(2,1)} %x_hbm.1, bf16[96,1024]{1,0:T(8,128)(2,1)} %mlp_hbm.1, bf16[1024,1024]{1,0:T(8,128)(2,1)} %w_hbm.1, f32[4,1024]{1,0:T(4,128)} %bias_hbm.1, bf16[4,1024,1024]{2,1,0:T(8,128)(2,1)} %v_hbm.1), custom_call_target="tpu_custom_call" | custom-call | tf_op jit(solution)/shard_map/exchange/pallas_call | solution.py:439
  115.7 4.7 %fusion = f32[1024,1024]{1,0:T(8,128)} fusion(bf16[384,1024]{1,0:T(8,128)(2,1)} %get-tuple-element.5, bf16[384,1024]{1,0:T(8,128)(2,1)} %get-tuple-element.6), kind=kOutput, calls=%fused_computation | convolution fusion | flops 805306368 | bytes 5767168 | tf_op jit(solution)/shard_map/dot_general | solution.py:478
  120.4 7.8 %copy.8 = bf16[4,1024,1024]{2,1,0:T(8,128)(2,1)} copy(bf16[4,1024,1024]{2,1,0:T(8,128)(2,1)} %get-tuple-element.11) | data formatting | bytes 16777216

commit v5 on v4

--- a/solution.py
+++ b/solution.py
@@ -273,6 +273,12 @@
 
     def produce(l, carry):
         bof[l] = back(l, o)
+
+        @pl.when(jnp.logical_and(t == layers - 1, l == t))
+        def _():
+            for k in both_down:
+                swap_sum(l, blk(k))
+
         for k in one_down:
             swap_sum(l, blk(k))
         bown[l] = back(l, y)
@@ -285,10 +291,6 @@
                 @pl.when(l < t)
                 def _():
                     send_both(l, b)
-
-                @pl.when(l == t)
-                def _():
-                    swap_sum(l, b)
 
         return carry
 
@@ -473,10 +475,58 @@
     )(layer_inputs, mlp_outputs, enc_weight, enc_bias, dec_weight)
 
 
+def finish_kernel(
+    xg_hbm, pg_hbm, dec_hbm, enc_out, dec_out, xg, pg, enc, dec, in_sem, dec_in, dec_sem, enc_sem
+):
+    layers = dec.shape[0]
+    piece = enc.shape[0] // layers
+    ins = [
+        pltpu.make_async_copy(xg_hbm, xg, in_sem.at[0]),
+        pltpu.make_async_copy(pg_hbm, pg, in_sem.at[1]),
+    ]
+    reads = [pltpu.make_async_copy(dec_hbm.at[l], dec.at[l], dec_in.at[l]) for l in range(layers)]
+    for copy in ins + reads:
+        copy.start()
+    for copy in ins:
+        copy.wait()
+    writes = []
+    for l in range(layers):
+        part = pl.ds(l * piece, piece)
+        enc[part, :] = lax.dot_general(
+            xg[:, part], pg[...], (((0,), (0,)), ((), ())), preferred_element_type=F32
+        )
+        writes.append(pltpu.make_async_copy(enc.at[part], enc_out.at[part], enc_sem.at[l]))
+        writes[-1].start()
+        reads[l].wait()
+        writes.append(pltpu.make_async_copy(dec.at[l], dec_out.at[l], dec_sem.at[l]))
+        writes[-1].start()
+    for copy in writes:
+        copy.wait()
+
+
 def local(layer_inputs, mlp_outputs, enc_weight, enc_bias, dec_weight):
-    dec_grad, xg, pg = exchange(layer_inputs, mlp_outputs, enc_weight, enc_bias, dec_weight)
-    enc_grad = lax.dot_general(xg, pg, (((0,), (0,)), ((), ())), preferred_element_type=F32)
-    return (enc_grad, dec_grad)
+    dec, xg, pg = exchange(layer_inputs, mlp_outputs, enc_weight, enc_bias, dec_weight)
+    hbm = pl.BlockSpec(memory_space=pltpu.HBM)
+    per_layer = pltpu.SemaphoreType.DMA((dec.shape[0],))
+    return pl.pallas_call(
+        finish_kernel,
+        in_specs=[hbm] * 3,
+        out_specs=(hbm,) * 2,
+        out_shape=(
+            jax.ShapeDtypeStruct(enc_weight.shape, F32),
+            jax.ShapeDtypeStruct(dec_weight.shape, BF16),
+        ),
+        scratch_shapes=[
+            pltpu.VMEM(xg.shape, BF16),
+            pltpu.VMEM(pg.shape, BF16),
+            pltpu.VMEM(enc_weight.shape, F32),
+            pltpu.VMEM(dec.shape, BF16),
+            pltpu.SemaphoreType.DMA((2,)),
+            per_layer, per_layer, per_layer,
+        ],
+        compiler_params=pltpu.CompilerParams(vmem_limit_bytes=56 * 2**20),
+        name="finish",
+    )(xg, pg, dec)
 
 
 def solution(mesh):

time: 128 us -> 124 us (0.969)
  Pallas kernels: 115 us -> 123 us
  local copies, waits for them, and re-layouts: 7.76 us -> 0 us
  matrix products: 4.68 us -> 0 us
    pallas_call x0 -> x1, Pallas kernels: none -> 8.4 us  [local(): pl.pallas_call(finish_kernel, in_specs=[hbm] * 3, out_specs=(hbm,) * 2, o...]
    unnamed x1 -> x0, local copies, waits for them, and re-layouts: 7.76 us -> none
    dot_general x1 -> x0, matrix products: 4.68 us -> none  [local(): lax.dot_general(xg, pg, (((0,), (0,)), ((), ())), preferred_element_type=...]
where the time goes in v5:
time: 124 us
  Pallas kernels  123 us (99%)
    pallas_call x1, Pallas kernels, exchange(): pl.pallas_call(functools.partial(exchange_kernel, layers, blocks, rscale)...  115 us
    pallas_call x1, Pallas kernels, local(): pl.pallas_call(finish_kernel, in_specs=[hbm] * 3, out_specs=(hbm,) * 2, o...  8.4 us

profile of v5, /device:TPU:20, one launch (start us, length us, event | category | flops | bytes accessed | tf_op | source)
XLA Modules:
  0.0 124.1 jit_solution(2128533481413663307)
XLA Ops:
  0.6 115.1 %exchange.1 = (bf16[4,1024,1024]{2,1,0:T(8,128)(2,1)}, bf16[384,1024]{1,0:T(8,128)(2,1)}, bf16[384,1024]{1,0:T(8,128)(2,1)}) custom-call(bf16[96,1024]{1,0:T(8,128)(2,1)} %x_hbm.1, bf16[96,1024]{1,0:T(8,128)(2,1)} %mlp_hbm.1, bf16[1024,1024]{1,0:T(8,128)(2,1)} %w_hbm.1, f32[4,1024]{1,0:T(4,128)} %bias_hbm.1, bf16[4,1024,1024]{2,1,0:T(8,128)(2,1)} %v_hbm.1), custom_call_target="tpu_custom_call" | custom-call | tf_op jit(solution)/shard_map/exchange/pallas_call | solution.py:441
  115.7 8.4 %finish.1 = (f32[1024,1024]{1,0:T(8,128)}, bf16[4,1024,1024]{2,1,0:T(8,128)(2,1)}) custom-call(bf16[384,1024]{1,0:T(8,128)(2,1)} %get-tuple-element.5.xg_hbm, bf16[384,1024]{1,0:T(8,128)(2,1)} %get-tuple-element.6.pg_hbm, bf16[4,1024,1024]{2,1,0:T(8,128)(2,1)} %get-tuple-element.7.dec_hbm), custom_call_target="tpu_custom_call" | custom-call | tf_op jit(solution)/shard_map/finish/pallas_call | solution.py:511

commit v6 on v5

--- a/solution.py
+++ b/solution.py
@@ -54,8 +54,8 @@
     v_copy = pltpu.make_async_copy(v_hbm, v, in_sem.at[4])
     for copy in (own_x, w_copy, bias_copy, mlp_copy, v_copy):
         copy.start()
-    both_up = list(range(blocks // 2, blocks))
-    one_up = list(range(blocks // 2))
+    both_up = list(range(blocks - max(blocks // 4, 1), blocks))
+    one_up = list(range(blocks - max(blocks // 4, 1)))
     both_down = list(range(blocks - max(blocks // 4, 1), blocks))
     one_down = list(range(blocks - max(blocks // 4, 1)))
 

time: 124 us -> 119 us (0.960)
  Pallas kernels: 123 us -> 118 us
    pallas_call x1, Pallas kernels: 115 us -> 110 us  [exchange(): pl.pallas_call(functools.partial(exchange_kernel, layers, blocks, rscale)...]
where the time goes in v6:
time: 119 us
  Pallas kernels  118 us (99%)
    pallas_call x1, Pallas kernels, exchange(): pl.pallas_call(functools.partial(exchange_kernel, layers, blocks, rscale)...  110 us
    pallas_call x1, Pallas kernels, local(): pl.pallas_call(finish_kernel, in_specs=[hbm] * 3, out_specs=(hbm,) * 2, o...  8.41 us

profile of v6, /device:TPU:20, one launch (start us, length us, event | category | flops | bytes accessed | tf_op | source)
XLA Modules:
  0.0 118.7 jit_solution(15190718925973886564)
XLA Ops:
  0.6 109.6 %exchange.1 = (bf16[4,1024,1024]{2,1,0:T(8,128)(2,1)}, bf16[384,1024]{1,0:T(8,128)(2,1)}, bf16[384,1024]{1,0:T(8,128)(2,1)}) custom-call(bf16[96,1024]{1,0:T(8,128)(2,1)} %x_hbm.1, bf16[96,1024]{1,0:T(8,128)(2,1)} %mlp_hbm.1, bf16[1024,1024]{1,0:T(8,128)(2,1)} %w_hbm.1, f32[4,1024]{1,0:T(4,128)} %bias_hbm.1, bf16[4,1024,1024]{2,1,0:T(8,128)(2,1)} %v_hbm.1), custom_call_target="tpu_custom_call" | custom-call | tf_op jit(solution)/shard_map/exchange/pallas_call | solution.py:441
  110.3 8.4 %finish.1 = (f32[1024,1024]{1,0:T(8,128)}, bf16[4,1024,1024]{2,1,0:T(8,128)(2,1)}) custom-call(bf16[384,1024]{1,0:T(8,128)(2,1)} %get-tuple-element.5.xg_hbm, bf16[384,1024]{1,0:T(8,128)(2,1)} %get-tuple-element.6.pg_hbm, bf16[4,1024,1024]{2,1,0:T(8,128)(2,1)} %get-tuple-element.7.dec_hbm), custom_call_target="tpu_custom_call" | custom-call | tf_op jit(solution)/shard_map/finish/pallas_call | solution.py:511
